TPU v7x, 32 devices: a whole 2x2x4 slice. The times are simulated.
32 devices in a mesh: groups: 2 (over x), frames: 16 (over z, y, core).
Axes of the slice: x: 2, y: 2, z: 4, core: 2. Of those that a mesh axis runs over, the one named last changes fastest.
Arguments:
- features: bfloat16 [4096, 1024], P(('groups', 'frames')), parts along dimension 0, may hold values from -6 to 6
- valid_length: int32 [2], P('groups'), parts along dimension 0, may hold values from 1024 to 2048
- ln1_gain: float32 [1024], replicated, may hold values from 0.5 to 1.5
- w_qkv: bfloat16 [1024, 1536], P('frames'), may hold values from -3 to 3
- w_out: bfloat16 [512, 1024], P('frames'), may hold values from -0.25 to 0.25
- ln2_gain: float32 [1024], replicated, may hold values from 0.5 to 1.5
- w_pw1: bfloat16 [1024, 2048], P('frames'), may hold values from -0.1875 to 0.1875
- w_dw: float32 [9, 1024], replicated, may hold values from -2 to 2
- bn_scale: float32 [1024], replicated, may hold values from 0.5 to 2
- bn_shift: float32 [1024], replicated, may hold values from -3 to 3
- w_pw2: bfloat16 [1024, 1024], P('frames'), may hold values from -0.1875 to 0.1875
Outputs:
- block_out: bfloat16 [4096, 1024], P(('groups', 'frames')), parts along dimension 0
There are 2 independent parts, one for each index of `groups`. A program takes and returns all parts, laid end to end along the dimension named above; an argument that names none is the same for every part. Nothing has to cross between parts.
All inputs are finite; a program needn't handle non-finite values.
Results may differ from a plain program's by a relative error of at most 0.0098.
Values may be sent and summed in bfloat16 or wider, within the bound.
No kernel may reach another device: no remote copies, remote signals or barrier semaphores. Data moves between devices by JAX's collectives and lax.ppermute only.
A program may use at most 128 MiB of HBM per device.

v0:
```python
import math
import jax
import jax.numpy as jnp
from jax import lax
from jax.sharding import PartitionSpec as P

HEADS = 4
HD = 128
EPSILON = 1e-05


def extended(cells, sides, width):
    for axis, dim in sides:
        count = lax.axis_size(axis)
        ends = count - 1
        head = lax.slice_in_dim(cells, 0, width, axis=dim)
        tail = lax.slice_in_dim(cells, cells.shape[dim] - width, cells.shape[dim], axis=dim)
        cells = jnp.concatenate(
            [
                lax.ppermute(tail, axis, [(i, (i + 1) % count) for i in range(ends)]),
                cells,
                lax.ppermute(head, axis, [((i + 1) % count, i) for i in range(ends)]),
            ],
            axis=dim,
        )
    return cells


def layer_norm(values, gain):
    values = values.astype(jnp.float32)
    mean = jnp.mean(values, axis=-1, keepdims=True)
    centred = values - mean
    variance = jnp.mean(centred * centred, axis=-1, keepdims=True)
    return (centred * lax.rsqrt(variance + EPSILON) * gain).astype(jnp.bfloat16)


def per_device(
    features, valid_length, ln1_gain, w_qkv, w_out, ln2_gain, w_pw1, w_dw, bn_scale, bn_shift, w_pw2
):
    limit = valid_length[0]
    local_rows = features.shape[0]
    width = features.shape[1]
    att_width = w_qkv.shape[1] // 3
    scale = 1.0 / math.sqrt(HD)
    tails = (
        lax.all_gather(w_out, "frames", axis=0, tiled=True),
        lax.all_gather(w_pw1, "frames", axis=0, tiled=True),
        lax.all_gather(w_pw2, "frames", axis=0, tiled=True),
    )
    full_out, full_pw1, full_pw2 = tails
    normed1 = layer_norm(features, ln1_gain)
    qkv = jnp.dot(
        normed1,
        lax.all_gather(w_qkv, "frames", axis=0, tiled=True),
        preferred_element_type=jnp.float32,
    ).astype(jnp.bfloat16)
    query_heads = qkv[:, :att_width].reshape(local_rows, HEADS, HD)
    keys = qkv[:, att_width : 2 * att_width]
    values = qkv[:, 2 * att_width :]
    maxima = jnp.full((HEADS, local_rows), -1e30, jnp.float32)
    key_rows = lax.all_gather(keys, "frames", axis=0, tiled=True)
    value_rows = lax.all_gather(values, "frames", axis=0, tiled=True)
    count = key_rows.shape[0]
    key_heads = key_rows.reshape(count, HEADS, HD)
    value_heads = value_rows.reshape(count, HEADS, HD)
    scores = (
        jnp.einsum("qhd,khd->hqk", query_heads, key_heads, preferred_element_type=jnp.float32)
        * scale
    )
    position = jnp.arange(count, dtype=jnp.int32)
    valid = (position < limit)[None, None, :]
    scores = jnp.where(valid, scores, -1e30)
    fresh = jnp.maximum(maxima, jnp.max(scores, axis=-1))
    weights = jnp.where(valid, jnp.exp(scores - fresh[..., None]), 0.0)
    totals = jnp.sum(weights, axis=-1)
    update = jnp.einsum(
        "hqk,khd->hqd",
        weights.astype(jnp.bfloat16),
        value_heads,
        preferred_element_type=jnp.float32,
    )
    summed = update
    maxima, totals, summed = (fresh, totals, summed)
    context = (
        (summed / totals[..., None])
        .transpose(1, 0, 2)
        .reshape(local_rows, att_width)
        .astype(jnp.bfloat16)
    )
    attended = features.astype(jnp.float32) + jnp.dot(
        context, full_out, preferred_element_type=jnp.float32
    )
    normed2 = layer_norm(attended, ln2_gain)
    both = jnp.dot(normed2, full_pw1, preferred_element_type=jnp.float32)
    frame_index = lax.axis_index("frames") * local_rows + jnp.arange(local_rows, dtype=jnp.int32)
    frame_valid = (frame_index < limit)[:, None]
    gated = jnp.where(frame_valid, both[:, :width] * jax.nn.sigmoid(both[:, width:]), 0.0).astype(
        jnp.bfloat16
    )
    half_window = (w_dw.shape[0] - 1) // 2
    widened = extended(gated, (("frames", 0),), half_window)
    widened = widened.astype(jnp.float32)
    conv = jnp.zeros((local_rows, width), jnp.float32)
    for tap in range(w_dw.shape[0]):
        conv = conv + w_dw[tap][None, :] * widened[tap : tap + local_rows]
    activated = jax.nn.silu(bn_scale * conv + bn_shift).astype(jnp.bfloat16)
    result = attended + jnp.dot(activated, full_pw2, preferred_element_type=jnp.float32)
    return result.astype(jnp.bfloat16)


def solution(mesh):
    placed = (
        P(("groups", "frames"), None),
        P("groups"),
        P(),
        P("frames", None),
        P("frames", None),
        P(),
        P("frames", None),
        P(),
        P(),
        P(),
        P("frames", None),
    )
    return jax.shard_map(
        per_device,
        mesh=mesh,
        in_specs=placed,
        out_specs=P(("groups", "frames"), None),
        check_vma=False,
    )
```

profile of v0, /device:TPU:0, one launch (start us, length us, event | category | flops | bytes accessed | tf_op | source)
XLA Modules:
  0.0 286.1 jit_solution(17644636704648669902)
XLA Ops:
  6.5 0.7 all-gather.7.cloned.1.call-update
  7.3 1.1 convert_reduce_fusion
  8.4 1.2 fusion.21
  9.6 48.0 %all-gather.7.cloned.1.call-done = bf16[1024,1536]{1,0:T(8,128)(2,1)} async-done(((bf16[64,1536]{1,0:T(8,128)(2,1)}), bf16[1024,1536]{1,0:T(8,128)(2,1)}) %all-gather.7.cloned.1.call-update) | async-done | bytes 3145744 | tf_op jit(solution)/shard_map/all_gather | solution.py:54
  57.6 2.6 convolution_convert_fusion
  60.2 0.7 slice_bitcast_fusion
  61.0 0.7 all-gather.9.cloned.1.call-update
  61.7 0.5 all-gather.13.cloned.1.call-update
  62.3 0.5 all-gather.15.cloned.1.call-update
  64.1 37.2 %all-gather.11.cloned.1.call-done = bf16[2048,512]{1,0:T(8,128)(2,1)} async-done(((bf16[128,512]{1,0:T(8,128)(2,1)}), bf16[2048,512]{1,0:T(8,128)(2,1)}) %all-gather.11.cloned.1.call-update) | async-done | bytes 2097168 | tf_op jit(solution)/shard_map/all_gather | solution.py:62
  101.3 2.9 %copy.15 = bf16[2048,512]{0,1:T(8,128)(2,1)S(1)} copy(bf16[2048,512]{1,0:T(8,128)(2,1)} %all-gather.11.cloned.1.call-done) | data formatting | bytes 4194304 | tf_op jit(solution)/shard_map/reshape | solution.py:65
  104.3 39.4 %all-gather.9.cloned.1.call-done = bf16[2048,512]{1,0:T(8,128)(2,1)} async-done(((bf16[128,512]{1,0:T(8,128)(2,1)}), bf16[2048,512]{1,0:T(8,128)(2,1)}) %all-gather.9.cloned.1.call-update) | async-done | bytes 2097168 | tf_op jit(solution)/shard_map/all_gather | solution.py:61
  143.7 2.5 fusion
  146.2 1.1 fusion.1
  147.3 1.3 fusion.16
  148.6 33.8 %all-gather.13.cloned.1.call-done = bf16[512,1024]{1,0:T(8,128)(2,1)} async-done(((bf16[32,1024]{1,0:T(8,128)(2,1)}), bf16[512,1024]{1,0:T(8,128)(2,1)}) %all-gather.13.cloned.1.call-update) | async-done | bytes 1048592 | tf_op jit(solution)/shard_map/all_gather | solution.py:46
  182.5 1.6 fusion.68
  184.4 49.6 %all-gather.15.cloned.1.call-done = bf16[1024,2048]{1,0:T(8,128)(2,1)} async-done(((bf16[64,2048]{1,0:T(8,128)(2,1)}), bf16[1024,2048]{1,0:T(8,128)(2,1)}) %all-gather.15.cloned.1.call-update) | async-done | bytes 4194320 | tf_op jit(solution)/shard_map/all_gather | solution.py:47
  234.0 3.0 %fusion.40 = f32[128,2048]{1,0:T(8,128)S(1)} fusion(bf16[1024,2048]{1,0:T(8,128)(2,1)} %all-gather.15.cloned.1.call-done, f32[128,1024]{1,0:T(8,128)S(1)} %get-tuple-element.22, f32[1024]{0:T(1024)S(1)} %copy-done.2, f32[128]{0:T(128)S(1)} %add_rsqrt_fusion, f32[128]{0:T(128)S(1)} %broadcast_multiply_fusion), kind=kOutput, calls=%fused_computation.54 | convolution fusion | flops 537395200 | bytes 5772288 | tf_op jit(solution)/shard_map/dot_general | solution.py:94
  237.1 2.2 collective-permute-start
  239.3 1.3 collective-permute-start.1
  240.7 1.7 collective-permute-done.1
  242.4 33.5 %all-gather.17.cloned.1.call-done = bf16[1024,1024]{1,0:T(8,128)(2,1)} async-done(((bf16[64,1024]{1,0:T(8,128)(2,1)}), bf16[1024,1024]{1,0:T(8,128)(2,1)}) %all-gather.17.cloned.1.call-update) | async-done | bytes 2097168 | tf_op jit(solution)/shard_map/all_gather | solution.py:48
  275.9 3.3 %fusion.9 = bf16[128,1024]{1,0:T(8,128)(2,1)} fusion(f32[128,1024]{1,0:T(8,128)S(1)} %get-tuple-element.22, bf16[1024,1024]{1,0:T(8,128)(2,1)} %all-gather.17.cloned.1.call-done, f32[136,1024]{1,0:T(8,128)S(1)} %maximum_convert_fusion, f32[1024]{0:T(1024)S(1)} %copy-done.3, f32[1024]{0:T(1024)S(1)} %bitcast.52, f32[1024]{0:T(1024)S(1)} %bitcast.53, ...), kind=kOutput, calls=%fused_computation.13 | convolution fusion | flops 271843328 | bytes 7647232 | tf_op jit(solution)/shard_map/dot_general | solution.py:107
  (31 shorter events, 1.3 us)
Async XLA Ops:
  6.5 51.0 %all-gather.7.cloned.1.call-start = ((), (), s32[]{:S(2)}) async-start(), calls=%async_computation | async-start | bytes 3342336 | tf_op jit(solution)/shard_map/all_gather | solution.py:54
  7.3 94.1 %all-gather.11.cloned.1.call-start = ((), (), s32[]{:S(2)}) async-start(), calls=%async_computation.2 | async-start | bytes 2228224 | tf_op jit(solution)/shard_map/all_gather | solution.py:62
  61.0 82.7 %all-gather.9.cloned.1.call-start = ((), (), s32[]{:S(2)}) async-start(), calls=%async_computation.1 | async-start | bytes 2228224 | tf_op jit(solution)/shard_map/all_gather | solution.py:61
  61.7 120.8 %all-gather.13.cloned.1.call-start = ((), (), s32[]{:S(2)}) async-start(), calls=%async_computation.3 | async-start | bytes 1114112 | tf_op jit(solution)/shard_map/all_gather | solution.py:46
  62.3 171.7 %all-gather.15.cloned.1.call-start = ((), (), s32[]{:S(2)}) async-start(), calls=%async_computation.4 | async-start | bytes 4456448 | tf_op jit(solution)/shard_map/all_gather | solution.py:47
  62.9 213.1 %all-gather.17.cloned.1.call-start = ((), (), s32[]{:S(2)}) async-start(), calls=%async_computation.5 | async-start | bytes 2228224 | tf_op jit(solution)/shard_map/all_gather | solution.py:48
  147.3 35.2 %copy-start = (bf16[128,1024]{1,0:T(8,128)(2,1)S(1)}, bf16[128,1024]{1,0:T(8,128)(2,1)}, u32[]{:S(2)}) copy-start(bf16[128,1024]{1,0:T(8,128)(2,1)} %param.11) | copy-start | bytes 786436
  147.3 86.7 %copy-start.2 = (f32[1024]{0:T(1024)S(1)}, f32[1024]{0:T(1024)}, u32[]{:S(2)}) copy-start(f32[1024]{0:T(1024)} %param.16) | copy-start | bytes 12292
  184.1 56.5 %copy-start.1 = (f32[9,1024]{1,0:T(8,128)S(1)}, f32[9,1024]{1,0:T(8,128)}, u32[]{:S(2)}) copy-start(f32[9,1024]{1,0:T(8,128)} %param.18) | copy-start | bytes 110596
  184.1 91.8 %copy-start.3 = (f32[1024]{0:T(1024)S(1)}, f32[1024]{0:T(1024)}, u32[]{:S(2)}) copy-start(f32[1024]{0:T(1024)} %param.20) | copy-start | bytes 12292
  184.1 91.8 %copy-start.4 = (f32[1024]{0:T(1024)S(1)}, f32[1024]{0:T(1024)}, u32[]{:S(2)}) copy-start(f32[1024]{0:T(1024)} %param.19) | copy-start | bytes 12292
  237.1 3.5 %collective-permute-start = (bf16[4,1024]{1,0:T(4,128)(2,1)S(1)}, bf16[4,1024]{1,0:T(4,128)(2,1)S(1)}, u32[]{:S(2)}, u32[]{:S(2)}) collective-permute-start(bf16[4,1024]{1,0:T(4,128)(2,1)S(1)} %get-tuple-element.8), channel_id=1, source_target_pairs={{0,1},{1,2},{2,3},{3,4},{4,5},{5,6},{6,7},{7,8},{8,9},{9,10},{10,1... | collective-permute-start | bytes 24584 | tf_op jit(solution)/shard_map/ppermute | solution.py:20
  239.3 3.1 %collective-permute-start.1 = (bf16[4,1024]{1,0:T(4,128)(2,1)S(1)}, bf16[4,1024]{1,0:T(4,128)(2,1)S(1)}, u32[]{:S(2)}, u32[]{:S(2)}) collective-permute-start(bf16[4,1024]{1,0:T(4,128)(2,1)S(1)} %get-tuple-element.9), channel_id=1, source_target_pairs={{1,0},{2,1},{3,2},{4,3},{5,4},{6,5},{7,6},{8,7},{9,8},{10,9},{11,1... | collective-permute-start | bytes 24584 | tf_op jit(solution)/shard_map/ppermute | solution.py:22
Sparse Core Ops, SparseCore 0:
  9.6 47.8 all-gather.6
  61.1 40.1 all-gather.10
  103.5 40.1 all-gather.8
  145.7 36.7 all-gather.12
  184.5 49.4 all-gather.14
  236.0 39.8 all-gather.16
where the time goes:
time: 287 us; the launch traced here: 286 us
  waiting for transfers between devices  246 us (86%)
  matrix products  14.4 us (5%)
  between operations  14.3 us (5%)
  other arithmetic  3.81 us (1%)
  local copies, waits for them, and re-layouts  3.71 us (1%)
  starting transfers between devices  3.65 us (1%)
    all_gather x1, waiting for transfers between devices, per_device(): lax.all_gather(w_pw1, 'frames', axis=0, tiled=True)  49.6 us
    all_gather x1, waiting for transfers between devices, per_device(): lax.all_gather(w_qkv, 'frames', axis=0, tiled=True)  48 us
    all_gather x1, waiting for transfers between devices, per_device(): key_rows = lax.all_gather(keys, 'frames', axis=0, tiled=True)  39.4 us
    all_gather x1, waiting for transfers between devices, per_device(): value_rows = lax.all_gather(values, 'frames', axis=0, tiled=True)  37.2 us
    all_gather x1, waiting for transfers between devices, per_device(): lax.all_gather(w_out, 'frames', axis=0, tiled=True)  33.8 us
    all_gather x1, waiting for transfers between devices, per_device(): lax.all_gather(w_pw2, 'frames', axis=0, tiled=True)  33.5 us
  transfers between devices with their start and end apart: 8, of which 7 were waited for; matrix products, arithmetic and copies ran while one was open for 5% of the time, Pallas kernels for 0%

commit v1 on v0

--- a/solution.py
+++ b/solution.py
@@ -58,8 +58,11 @@
     keys = qkv[:, att_width : 2 * att_width]
     values = qkv[:, 2 * att_width :]
     maxima = jnp.full((HEADS, local_rows), -1e30, jnp.float32)
-    key_rows = lax.all_gather(keys, "frames", axis=0, tiled=True)
-    value_rows = lax.all_gather(values, "frames", axis=0, tiled=True)
+    key_rows, value_rows = jnp.split(
+        lax.all_gather(jnp.concatenate([keys, values], axis=1), "frames", axis=0, tiled=True),
+        [keys.shape[1]],
+        axis=1,
+    )
     count = key_rows.shape[0]
     key_heads = key_rows.reshape(count, HEADS, HD)
     value_heads = value_rows.reshape(count, HEADS, HD)

time: 287 us -> 253 us (0.88)
  waiting for transfers between devices: 246 us -> 208 us
  local copies, waits for them, and re-layouts: 3.71 us -> 7.28 us
    all_gather x2 -> x1, waiting for transfers between devices: 76.6 us -> 46.9 us  [per_device(): lax.all_gather(jnp.concatenate([keys, values], axis=1), 'frames', axis=0,...]
    all_gather x1, waiting for transfers between devices: 33.8 us -> 27.1 us  [per_device(): lax.all_gather(w_out, 'frames', axis=0, tiled=True)]
    unnamed x11 -> x13, local copies, waits for them, and re-layouts: 0.74 us -> 4.04 us
  transfers between devices with their start and end apart: 8 -> 7, of which waited for: 7 -> 6; matrix products, arithmetic and copies ran while one was open for 5% -> 7% of each run, Pallas kernels for 0% -> 0%
where the time goes in v1:
time: 253 us; the launch traced here: 252 us
  waiting for transfers between devices  208 us (82%)
  matrix products  14.5 us (6%)
  between operations  14 us (6%)
  local copies, waits for them, and re-layouts  7.28 us (3%)
  starting transfers between devices  4.48 us (2%)
  other arithmetic  3.81 us (2%)
    all_gather x1, waiting for transfers between devices, per_device(): lax.all_gather(w_pw1, 'frames', axis=0, tiled=True)  49.6 us
    all_gather x1, waiting for transfers between devices, per_device(): lax.all_gather(w_qkv, 'frames', axis=0, tiled=True)  48 us
    all_gather x1, waiting for transfers between devices, per_device(): lax.all_gather(jnp.concatenate([keys, values], axis=1), 'frames', axis=0,...  46.9 us
    all_gather x1, waiting for transfers between devices, per_device(): lax.all_gather(w_pw2, 'frames', axis=0, tiled=True)  33.5 us
    all_gather x1, waiting for transfers between devices, per_device(): lax.all_gather(w_out, 'frames', axis=0, tiled=True)  27.1 us
  transfers between devices with their start and end apart: 7, of which 6 were waited for; matrix products, arithmetic and copies ran while one was open for 7% of the time, Pallas kernels for 0%

profile of v1, /device:TPU:0, one launch (start us, length us, event | category | flops | bytes accessed | tf_op | source)
XLA Modules:
  0.0 252.4 jit_solution(2929440256516899960)
XLA Ops:
  6.5 0.7 all-gather.6.cloned.1.call-update
  7.3 1.1 convert_reduce_fusion
  8.4 1.2 fusion.21
  9.6 48.0 %all-gather.6.cloned.1.call-done = bf16[1024,1536]{1,0:T(8,128)(2,1)} async-done(((bf16[64,1536]{1,0:T(8,128)(2,1)}), bf16[1024,1536]{1,0:T(8,128)(2,1)}) %all-gather.6.cloned.1.call-update) | async-done | bytes 3145744 | tf_op jit(solution)/shard_map/all_gather | solution.py:54
  57.6 2.6 %convolution_convert_fusion = bf16[128,1536]{1,0:T(8,128)(2,1)S(1)} fusion(bf16[1024,1536]{1,0:T(8,128)(2,1)} %all-gather.6.cloned.1.call-done, bf16[128,1024]{1,0:T(8,128)(2,1)} %param.11, f32[1024]{0:T(1024)} %param.13, f32[128]{0:T(128)S(1)} %add_rsqrt_fusion.1, f32[128]{0:T(128)S(1)} %broadcast_multiply_fusion.1), kind=kOutput, calls=%fused_computation.5 | convolution fusion | flops 403505152 | bytes 3806208 | tf_op jit(solution)/shard_map/dot_general | solution.py:52
  60.2 0.7 concatenate.8
  61.0 0.7 all-gather.10.cloned.1.call-update
  61.8 0.5 all-gather.12.cloned.1.call-update
  62.3 0.5 all-gather.14.cloned.1.call-update
  63.6 46.9 %all-gather.8.cloned.1.call-done = bf16[2048,1024]{1,0:T(8,128)(2,1)} async-done(((bf16[128,1024]{1,0:T(8,128)(2,1)}), bf16[2048,1024]{1,0:T(8,128)(2,1)}) %all-gather.8.cloned.1.call-update) | async-done | bytes 4194320 | tf_op jit(solution)/shard_map/all_gather | solution.py:62
  110.5 4.0 %slice_bitcast_fusion = (bf16[256,4,8,128]{3,2,1,0:T(8,128)(2,1)}, bf16[2048,512]{1,0:T(8,128)(2,1)S(1)}) fusion(bf16[2048,1024]{1,0:T(8,128)(2,1)} %all-gather.8.cloned.1.call-done), kind=kLoop, calls=%fused_computation.9 | loop fusion | bytes 8388608
  114.5 2.5 copy.15
  117.0 2.7 %fusion = (f32[4,128]{1,0:T(4,128)S(1)}, f32[4,128,2048]{2,1,0:T(8,128)S(1)}) fusion(pred[2048]{0:T(1024)(128)(4,1)S(1)} %iota_compare_fusion, bf16[256,4,8,128]{3,2,1,0:T(8,128)(2,1)} %get-tuple-element.5, bf16[128,1536]{1,0:T(8,128)(2,1)S(1)} %convolution_convert_fusion), kind=kOutput, calls=%fused_computation.2 | convolution fusion | flops 271580672 | bytes 6426624 | tf_op jit(solution)/shard_map/qhd,khd->hqk/dot_general | solution.py:70
  119.7 1.1 fusion.1
  120.8 1.3 fusion.16
  122.1 27.1 %all-gather.10.cloned.1.call-done = bf16[512,1024]{1,0:T(8,128)(2,1)} async-done(((bf16[32,1024]{1,0:T(8,128)(2,1)}), bf16[512,1024]{1,0:T(8,128)(2,1)}) %all-gather.10.cloned.1.call-update) | async-done | bytes 1048592 | tf_op jit(solution)/shard_map/all_gather | solution.py:46
  149.2 1.6 fusion.68
  151.0 49.6 %all-gather.12.cloned.1.call-done = bf16[1024,2048]{1,0:T(8,128)(2,1)} async-done(((bf16[64,2048]{1,0:T(8,128)(2,1)}), bf16[1024,2048]{1,0:T(8,128)(2,1)}) %all-gather.12.cloned.1.call-update) | async-done | bytes 4194320 | tf_op jit(solution)/shard_map/all_gather | solution.py:47
  200.7 3.0 %fusion.40 = f32[128,2048]{1,0:T(8,128)S(1)} fusion(bf16[1024,2048]{1,0:T(8,128)(2,1)} %all-gather.12.cloned.1.call-done, f32[128,1024]{1,0:T(8,128)S(1)} %get-tuple-element.21, f32[1024]{0:T(1024)S(1)} %copy-done.3, f32[128]{0:T(128)S(1)} %add_rsqrt_fusion, f32[128]{0:T(128)S(1)} %broadcast_multiply_fusion), kind=kOutput, calls=%fused_computation.55 | convolution fusion | flops 537395200 | bytes 5772288 | tf_op jit(solution)/shard_map/dot_general | solution.py:97
  203.8 1.3 collective-permute-start.1
  205.1 3.0 %collective-permute-start = (bf16[4,1024]{1,0:T(4,128)(2,1)S(1)}, bf16[4,1024]{1,0:T(4,128)(2,1)S(1)}, u32[]{:S(2)}, u32[]{:S(2)}) collective-permute-start(bf16[4,1024]{1,0:T(4,128)(2,1)S(1)} %get-tuple-element.7), channel_id=1, source_target_pairs={{0,1},{1,2},{2,3},{3,4},{4,5},{5,6},{6,7},{7,8},{8,9},{9,10},{10,1... | collective-permute-start | bytes 24584 | tf_op jit(solution)/shard_map/ppermute | solution.py:20
  208.2 0.8 collective-permute-done
  209.1 33.5 %all-gather.14.cloned.1.call-done = bf16[1024,1024]{1,0:T(8,128)(2,1)} async-done(((bf16[64,1024]{1,0:T(8,128)(2,1)}), bf16[1024,1024]{1,0:T(8,128)(2,1)}) %all-gather.14.cloned.1.call-update) | async-done | bytes 2097168 | tf_op jit(solution)/shard_map/all_gather | solution.py:48
  242.6 3.3 %fusion.9 = bf16[128,1024]{1,0:T(8,128)(2,1)} fusion(f32[128,1024]{1,0:T(8,128)S(1)} %get-tuple-element.21, bf16[1024,1024]{1,0:T(8,128)(2,1)} %all-gather.14.cloned.1.call-done, f32[136,1024]{1,0:T(8,128)S(1)} %maximum_convert_fusion, f32[1024]{0:T(1024)S(1)} %copy-done.4, f32[1024]{0:T(1024)S(1)} %bitcast.52, f32[1024]{0:T(1024)S(1)} %bitcast.53, ...), kind=kOutput, calls=%fused_computation.14 | convolution fusion | flops 271843328 | bytes 7647232 | tf_op jit(solution)/shard_map/dot_general | solution.py:110
  (31 shorter events, 0.7 us)
Async XLA Ops:
  6.5 51.0 %all-gather.6.cloned.1.call-start = ((), (), s32[]{:S(2)}) async-start(), calls=%async_computation | async-start | bytes 3342336 | tf_op jit(solution)/shard_map/all_gather | solution.py:54
  7.3 103.2 %all-gather.8.cloned.1.call-start = ((), (), s32[]{:S(2)}) async-start(), calls=%async_computation.1 | async-start | bytes 4456448 | tf_op jit(solution)/shard_map/all_gather | solution.py:62
  61.0 88.2 %all-gather.10.cloned.1.call-start = ((), (), s32[]{:S(2)}) async-start(), calls=%async_computation.2 | async-start | bytes 1114112 | tf_op jit(solution)/shard_map/all_gather | solution.py:46
  61.7 139.0 %all-gather.12.cloned.1.call-start = ((), (), s32[]{:S(2)}) async-start(), calls=%async_computation.3 | async-start | bytes 4456448 | tf_op jit(solution)/shard_map/all_gather | solution.py:47
  62.3 180.3 %all-gather.14.cloned.1.call-start = ((), (), s32[]{:S(2)}) async-start(), calls=%async_computation.4 | async-start | bytes 2228224 | tf_op jit(solution)/shard_map/all_gather | solution.py:48
  117.0 3.8 %copy-start.1 = (bf16[2048,512]{0,1:T(8,128)(2,1)S(1)}, bf16[2048,512]{0,1:T(8,128)(2,1)}, u32[]{:S(2)}) copy-start(bf16[2048,512]{0,1:T(8,128)(2,1)} %copy.15) | copy-start | bytes 6291460
  120.8 28.4 %copy-start = (bf16[128,1024]{1,0:T(8,128)(2,1)S(1)}, bf16[128,1024]{1,0:T(8,128)(2,1)}, u32[]{:S(2)}) copy-start(bf16[128,1024]{1,0:T(8,128)(2,1)} %param.11) | copy-start | bytes 786436
  120.8 79.9 %copy-start.3 = (f32[1024]{0:T(1024)S(1)}, f32[1024]{0:T(1024)}, u32[]{:S(2)}) copy-start(f32[1024]{0:T(1024)} %param.16) | copy-start | bytes 12292
  150.8 57.4 %copy-start.2 = (f32[9,1024]{1,0:T(8,128)S(1)}, f32[9,1024]{1,0:T(8,128)}, u32[]{:S(2)}) copy-start(f32[9,1024]{1,0:T(8,128)} %param.18) | copy-start | bytes 110596
  150.8 91.7 %copy-start.4 = (f32[1024]{0:T(1024)S(1)}, f32[1024]{0:T(1024)}, u32[]{:S(2)}) copy-start(f32[1024]{0:T(1024)} %param.20) | copy-start | bytes 12292
  150.8 91.7 %copy-start.5 = (f32[1024]{0:T(1024)S(1)}, f32[1024]{0:T(1024)}, u32[]{:S(2)}) copy-start(f32[1024]{0:T(1024)} %param.19) | copy-start | bytes 12292
  203.8 4.4 %collective-permute-start.1 = (bf16[4,1024]{1,0:T(4,128)(2,1)S(1)}, bf16[4,1024]{1,0:T(4,128)(2,1)S(1)}, u32[]{:S(2)}, u32[]{:S(2)}) collective-permute-start(bf16[4,1024]{1,0:T(4,128)(2,1)S(1)} %get-tuple-element.8), channel_id=1, source_target_pairs={{1,0},{2,1},{3,2},{4,3},{5,4},{6,5},{7,6},{8,7},{9,8},{10,9},{11,1... | collective-permute-start | bytes 24584 | tf_op jit(solution)/shard_map/ppermute | solution.py:22
  205.1 3.8 %collective-permute-start = (bf16[4,1024]{1,0:T(4,128)(2,1)S(1)}, bf16[4,1024]{1,0:T(4,128)(2,1)S(1)}, u32[]{:S(2)}, u32[]{:S(2)}) collective-permute-start(bf16[4,1024]{1,0:T(4,128)(2,1)S(1)} %get-tuple-element.7), channel_id=1, source_target_pairs={{0,1},{1,2},{2,3},{3,4},{4,5},{5,6},{6,7},{7,8},{8,9},{9,10},{10,1... | collective-permute-start | bytes 24584 | tf_op jit(solution)/shard_map/ppermute | solution.py:20
Sparse Core Ops, SparseCore 0:
  9.6 47.8 all-gather.5
  61.1 49.3 all-gather.7
  112.7 36.4 all-gather.9
  151.2 49.4 all-gather.11
  202.7 39.8 all-gather.13
